TPU v7x, 512 devices: a whole 4x8x8 slice. The times are simulated.
512 devices in a mesh: blk: 32 (over x, y_lo, core), fsdp: 16 (over z, y_hi).
Axes of the slice: x: 4, y: 8 (y_hi: 2, y_lo: 4; y = y_hi * 4 + y_lo), z: 8, core: 2. Of those that a mesh axis runs over, the one named last changes fastest.
Arguments:
- decoder_states: bfloat16 [8192, 4096], P('blk', 'fsdp'), may hold values from -10 to 10
- w_query: bfloat16 [4096, 4096], P('blk', 'fsdp'), may hold values from -0.09375 to 0.09375
- w_out_t: bfloat16 [4096, 4096], P('blk', 'fsdp'), may hold values from -0.1875 to 0.1875
- enc_keys: bfloat16 [8192, 4096], P('blk', 'fsdp'), may hold values from -80 to 80
- enc_values: bfloat16 [8192, 4096], P('blk', 'fsdp'), may hold values from -6 to 6
Outputs:
- attended: bfloat16 [8192, 4096], P(('blk', 'fsdp'))
All inputs are finite; a program needn't handle non-finite values.
Results may differ from a plain program's by a relative error of at most 0.0095.
Values may be sent and summed in bfloat16 or wider, within the bound.
A program may use at most 128 MiB of HBM per device.

v0:
```python
import math
import jax
import jax.numpy as jnp
from jax import lax
from jax.sharding import PartitionSpec as P

HEAD_DIM = 64


def absorb(fold_state, query_heads, key_rows, value_rows):
    running_top, running_sum, weighted = fold_state
    local_heads = query_heads.shape[1]
    key_heads = key_rows.reshape(key_rows.shape[0], local_heads, HEAD_DIM)
    value_heads = value_rows.reshape(value_rows.shape[0], local_heads, HEAD_DIM)
    scores = jnp.einsum(
        "qhd,khd->hqk", query_heads, key_heads, preferred_element_type=jnp.float32
    ) * (1.0 / math.sqrt(HEAD_DIM))
    new_top = jnp.max(scores, axis=2)
    rescale = jnp.exp(running_top - new_top)
    probability = jnp.exp(scores - new_top[:, :, None])
    running_sum = running_sum * rescale + jnp.sum(probability, axis=2)
    weighted = weighted * rescale[:, :, None] + jnp.einsum(
        "hqk,khd->hqd",
        probability.astype(jnp.bfloat16),
        value_heads,
        preferred_element_type=jnp.float32,
    )
    return (new_top, running_sum, weighted)


def shards(decoder_states, w_query, w_out_t, enc_keys, enc_values):
    query_full = lax.all_gather(w_query, "blk", axis=0, tiled=True)
    row_count = decoder_states.shape[0]
    columns = query_full.shape[1]
    local_heads = columns // HEAD_DIM
    queries = jnp.dot(
        lax.all_gather(decoder_states, "fsdp", axis=1, tiled=True),
        query_full,
        preferred_element_type=jnp.float32,
    ).astype(jnp.bfloat16)
    start_state = (
        jnp.full((local_heads, row_count), -jnp.inf, jnp.float32),
        jnp.zeros((local_heads, row_count), jnp.float32),
        jnp.zeros((local_heads, row_count, HEAD_DIM), jnp.float32),
    )
    query_heads = queries.reshape(row_count, local_heads, HEAD_DIM)
    final_state = absorb(
        start_state,
        query_heads,
        lax.all_gather(enc_keys, "blk", axis=0, tiled=True),
        lax.all_gather(enc_values, "blk", axis=0, tiled=True),
    )
    context = final_state[2] / final_state[1][:, :, None]
    context = jnp.transpose(context, (1, 0, 2)).reshape(row_count, columns).astype(jnp.bfloat16)
    out_full = lax.all_gather(w_out_t, "blk", axis=0, tiled=True)
    return lax.psum_scatter(
        lax.dot_general(
            context, out_full, (((1,), (1,)), ((), ())), preferred_element_type=jnp.float32
        ),
        "fsdp",
        scatter_dimension=0,
        tiled=True,
    ).astype(jnp.bfloat16)


def solution(mesh):
    in_specs = (
        P("blk", "fsdp"),
        P("blk", "fsdp"),
        P("blk", "fsdp"),
        P("blk", "fsdp"),
        P("blk", "fsdp"),
    )
    out_specs = P(("blk", "fsdp"), None)
    return jax.shard_map(shards, mesh=mesh, in_specs=in_specs, out_specs=out_specs, check_vma=False)
```

profile of v0, /device:TPU:8, one launch (start us, length us, event | category | flops | bytes accessed | tf_op | source)
XLA Modules:
  0.0 624.3 jit_solution(10942586508582458863)
XLA Ops:
  6.5 0.7 all-gather.6.cloned.1.call-update
  7.3 0.0 all-gather.8.cloned.1.call-start
  7.3 0.7 all-gather.8.cloned.1.call-update
  8.0 0.0 all-gather.10.cloned.1.call-start
  8.1 0.7 all-gather.10.cloned.1.call-update
  8.7 0.0 all-gather.12.cloned.1.call-start
  8.8 0.5 all-gather.12.cloned.1.call-update
  9.3 0.0 all-gather.14.cloned.1.call-start
  9.4 0.5 all-gather.14.cloned.1.call-update
  9.9 0.0 reduce-scatter.2.cloned.1.call-start
  10.0 110.0 %all-gather.6.cloned.1.call-done = bf16[256,4096]{1,0:T(8,128)(2,1)} async-done(((bf16[256,256]{1,0:T(8,128)(2,1)}), bf16[256,4096]{1,0:T(8,128)(2,1)}) %all-gather.6.cloned.1.call-update) | async-done | bytes 2097168 | tf_op jit(solution)/shard_map/all_gather | solution.py:37
  120.0 59.1 %all-gather.8.cloned.1.call-done = bf16[4096,256]{1,0:T(8,128)(2,1)} async-done(((bf16[128,256]{1,0:T(8,128)(2,1)}), bf16[4096,256]{1,0:T(8,128)(2,1)}) %all-gather.8.cloned.1.call-update) | async-done | bytes 2097168 | tf_op jit(solution)/shard_map/all_gather | solution.py:32
  179.0 3.1 convolution_convert_fusion
  182.2 63.7 %all-gather.10.cloned.1.call-done = bf16[8192,256]{1,0:T(8,128)(2,1)} async-done(((bf16[256,256]{1,0:T(8,128)(2,1)}), bf16[8192,256]{1,0:T(8,128)(2,1)}) %all-gather.10.cloned.1.call-update) | async-done | bytes 4194320 | tf_op jit(solution)/shard_map/all_gather | solution.py:50
  245.9 6.4 %copy.6 = bf16[8192,256]{0,1:T(8,128)(2,1)} copy(bf16[8192,256]{1,0:T(8,128)(2,1)} %all-gather.10.cloned.1.call-done) | data formatting | bytes 8388608 | tf_op jit(solution)/shard_map/all_gather | solution.py:50
  252.3 15.5 %multiply_reduce_fusion = (f32[4,256]{1,0:T(4,128)S(1)}, f32[4,256,8192]{2,1,0:T(8,128)}) fusion(bf16[256,4,64]{0,2,1:T(8,128)(2,1)S(1)} %bitcast.27, bf16[8192,4,64]{0,2,1:T(8,128)(2,1)} %bitcast.26), kind=kOutput, calls=%fused_computation.1 | convolution fusion | flops 1090518016 | bytes 37883904 | tf_op jit(solution)/shard_map/qhd,khd->hqk/dot_general | solution.py:15
  267.8 44.6 %all-gather.12.cloned.1.call-done = bf16[8192,256]{1,0:T(8,128)(2,1)} async-done(((bf16[256,256]{1,0:T(8,128)(2,1)}), bf16[8192,256]{1,0:T(8,128)(2,1)}) %all-gather.12.cloned.1.call-update) | async-done | bytes 4194320 | tf_op jit(solution)/shard_map/all_gather | solution.py:51
  312.4 6.4 %copy.7 = bf16[8192,256]{0,1:T(8,128)(2,1)} copy(bf16[8192,256]{1,0:T(8,128)(2,1)} %all-gather.12.cloned.1.call-done) | data formatting | bytes 8388608 | tf_op jit(solution)/shard_map/all_gather | solution.py:51
  318.8 14.1 %fusion = f32[4,256]{1,0:T(4,128)S(1)} fusion(f32[4,256,8192]{2,1,0:T(8,128)} %get-tuple-element.6, f32[4,256]{1,0:T(4,128)S(1)} %get-tuple-element.5), kind=kLoop, calls=%fused_computation.2 | loop fusion | flops 25164800 | bytes 33562624 | tf_op jit(solution)/shard_map/reduce_sum | solution.py:21
  332.9 15.5 %fusion.13 = bf16[256,4,64]{0,2,1:T(8,128)(2,1)S(1)} fusion(bf16[8192,4,64]{0,2,1:T(8,128)(2,1)} %bitcast.25, f32[4,256,8192]{2,1,0:T(8,128)} %get-tuple-element.6, f32[4,256]{1,0:T(4,128)S(1)} %get-tuple-element.5, f32[256,4]{0,1:T(4,128)S(1)} %bitcast_add_fusion, f32[256,4]{0,1:T(4,128)S(1)} %multiply_bitcast_fusion), kind=kOutput, calls=%fused_computation.9 | convolution fusion | flops 1099104256 | bytes 37892096 | tf_op jit(solution)/shard_map/hqk,khd->hqd/dot_general | solution.py:22
  348.5 27.8 %all-gather.14.cloned.1.call-done = bf16[4096,256]{1,0:T(8,128)(2,1)} async-done(((bf16[128,256]{1,0:T(8,128)(2,1)}), bf16[4096,256]{1,0:T(8,128)(2,1)}) %all-gather.14.cloned.1.call-update) | async-done | bytes 2097168 | tf_op jit(solution)/shard_map/all_gather | solution.py:55
  376.3 4.3 fusion.17
  380.6 235.3 %reduce-scatter.2.cloned.1.call-done = f32[16,4096]{1,0:T(8,128)} async-done(((f32[256,4096]{1,0:T(8,128)}), f32[16,4096]{1,0:T(8,128)}) %reduce-scatter.2.cloned.1.call-update) | async-done | bytes 262160 | tf_op jit(solution)/shard_map/reduce_scatter | solution.py:56
  615.8 1.6 convert_element_type.19
  (4 shorter events, 0.0 us)
Async XLA Ops:
  6.5 113.4 %all-gather.6.cloned.1.call-start = ((), (), s32[]{:S(2)}) async-start(), calls=%async_computation.1 | async-start | bytes 2228224 | tf_op jit(solution)/shard_map/all_gather | solution.py:37
  7.3 171.8 %all-gather.8.cloned.1.call-start = ((), (), s32[]{:S(2)}) async-start(), calls=%async_computation.2 | async-start | bytes 2162688 | tf_op jit(solution)/shard_map/all_gather | solution.py:32
  8.0 237.8 %all-gather.10.cloned.1.call-start = ((), (), s32[]{:S(2)}) async-start(), calls=%async_computation.3 | async-start | bytes 4325376 | tf_op jit(solution)/shard_map/all_gather | solution.py:50
  8.7 303.7 %all-gather.12.cloned.1.call-start = ((), (), s32[]{:S(2)}) async-start(), calls=%async_computation.4 | async-start | bytes 4325376 | tf_op jit(solution)/shard_map/all_gather | solution.py:51
  9.3 366.9 %all-gather.14.cloned.1.call-start = ((), (), s32[]{:S(2)}) async-start(), calls=%async_computation.5 | async-start | bytes 2162688 | tf_op jit(solution)/shard_map/all_gather | solution.py:55
  9.9 605.9 %reduce-scatter.2.cloned.1.call-start = ((), (), s32[]{:S(2)}) async-start(), calls=%async_computation.6 | async-start | bytes 4456448 | tf_op jit(solution)/shard_map/reduce_scatter | solution.py:56
Sparse Core Ops, SparseCore 0:
  10.4 109.5 all-gather.5
  122.1 56.8 all-gather.7
  181.2 64.6 all-gather.9
  247.9 64.5 all-gather.11
  314.4 61.7 all-gather.13
  380.7 235.0 reduce-scatter.1
where the time goes:
time: 625 us; the launch traced here: 624 us
  waiting for transfers between devices  544 us (87%)
  matrix products  38.5 us (6%)
  other arithmetic  15.7 us (3%)
  between operations  13.5 us (2%)
  local copies, waits for them, and re-layouts  12.8 us (2%)
    reduce_scatter x1, waiting for transfers between devices, shards(): lax.psum_scatter(lax.dot_general(context, out_full, (((1,), (1,)), ((), (...  235 us
    all_gather x1, waiting for transfers between devices, shards(): lax.all_gather(decoder_states, 'fsdp', axis=1, tiled=True)  110 us
    all_gather x1, waiting for transfers between devices, shards(): lax.all_gather(enc_keys, 'blk', axis=0, tiled=True)  63.7 us
    all_gather x1, waiting for transfers between devices, shards(): query_full = lax.all_gather(w_query, 'blk', axis=0, tiled=True)  59.1 us
    all_gather x1, waiting for transfers between devices, shards(): lax.all_gather(enc_values, 'blk', axis=0, tiled=True)  44.6 us
    all_gather x1, waiting for transfers between devices, shards(): out_full = lax.all_gather(w_out_t, 'blk', axis=0, tiled=True)  27.8 us
    dot_general x1, matrix products, absorb(): jnp.einsum('hqk,khd->hqd', probability.astype(jnp.bfloat16), value_heads,...  15.5 us
    dot_general x1, matrix products, absorb(): jnp.einsum('qhd,khd->hqk', query_heads, key_heads, preferred_element_type...  15.5 us
  transfers between devices with their start and end apart: 6, of which 6 were waited for; matrix products, arithmetic and copies ran while one was open for 10% of the time, Pallas kernels for 0%

commit v1 on v0

--- a/solution.py
+++ b/solution.py
@@ -29,7 +29,9 @@
 
 
 def shards(decoder_states, w_query, w_out_t, enc_keys, enc_values):
-    query_full = lax.all_gather(w_query, "blk", axis=0, tiled=True)
+    query_full = jnp.concatenate(
+        lax.all_to_all(jnp.stack([w_query] * lax.axis_size("blk")), "blk", 0, 0), axis=0
+    )
     row_count = decoder_states.shape[0]
     columns = query_full.shape[1]
     local_heads = columns // HEAD_DIM

time: 625 us -> 570 us (0.912)
  waiting for transfers between devices: 544 us -> 477 us
  starting transfers between devices: 0.19 us -> 9.65 us
    all_gather x1 -> x0, waiting for transfers between devices: 59.1 us -> none  [shards(): query_full = lax.all_gather(w_query, 'blk', axis=0, tiled=True)]
    all_to_all x0 -> x1, starting transfers between devices: none -> 9.49 us  [shards(): lax.all_to_all(jnp.stack([w_query] * lax.axis_size('blk')), 'blk', 0, 0)]
  transfers between devices with their start and end apart: 6 -> 6, of which waited for: 6 -> 5; matrix products, arithmetic and copies ran while one was open for 10% -> 11% of each run, Pallas kernels for 0% -> 0%
where the time goes in v1:
time: 570 us; the launch traced here: 569 us
  waiting for transfers between devices  477 us (84%)
  matrix products  37.9 us (7%)
  other arithmetic  15.7 us (3%)
  local copies, waits for them, and re-layouts  15.2 us (3%)
  between operations  13.2 us (2%)
  starting transfers between devices  9.65 us (2%)
    reduce_scatter x1, waiting for transfers between devices, shards(): lax.psum_scatter(lax.dot_general(context, out_full, (((1,), (1,)), ((), (...  239 us
    all_gather x1, waiting for transfers between devices, shards(): lax.all_gather(decoder_states, 'fsdp', axis=1, tiled=True)  104 us
    all_gather x1, waiting for transfers between devices, shards(): lax.all_gather(enc_keys, 'blk', axis=0, tiled=True)  59.3 us
    all_gather x1, waiting for transfers between devices, shards(): lax.all_gather(enc_values, 'blk', axis=0, tiled=True)  44.8 us
    all_gather x1, waiting for transfers between devices, shards(): out_full = lax.all_gather(w_out_t, 'blk', axis=0, tiled=True)  27.8 us
    dot_general x1, matrix products, absorb(): jnp.einsum('qhd,khd->hqk', query_heads, key_heads, preferred_element_type...  15.6 us
    dot_general x1, matrix products, absorb(): jnp.einsum('hqk,khd->hqd', probability.astype(jnp.bfloat16), value_heads,...  15.5 us
    reduce_sum x1, other arithmetic, absorb(): running_sum = running_sum * rescale + jnp.sum(probability, axis=2)  14.1 us
  transfers between devices with their start and end apart: 6, of which 5 were waited for; matrix products, arithmetic and copies ran while one was open for 11% of the time, Pallas kernels for 0%

profile of v1, /device:TPU:8, one launch (start us, length us, event | category | flops | bytes accessed | tf_op | source)
XLA Modules:
  0.0 569.0 jit_solution(4697451843141418027)
XLA Ops:
  6.5 0.7 all-gather.5.cloned.1.call-update
  7.3 0.0 all-gather.7.cloned.1.call-start
  7.3 0.7 all-gather.7.cloned.1.call-update
  8.0 0.0 all-gather.9.cloned.1.call-start
  8.1 0.7 all-gather.9.cloned.1.call-update
  8.7 2.4 stack.2
  11.1 9.5 %all-to-all-start = ((bf16[32,128,256]{2,1,0:T(8,128)(2,1)}), bf16[32,128,256]{2,1,0:T(8,128)(2,1)S(1)}, u32[]{:S(2)}, u32[]{:S(2)}) async-start(bf16[32,128,256]{2,1,0:T(8,128)(2,1)} %stack.2), calls=%async_computation | async-start | bytes 4194304 | tf_op jit(solution)/shard_map/all_to_all | solution.py:33
  20.6 0.0 all-gather.11.cloned.1.call-start
  20.7 0.5 all-gather.11.cloned.1.call-update
  21.2 0.0 reduce-scatter.2.cloned.1.call-start
  21.3 103.9 %all-gather.5.cloned.1.call-done = bf16[256,4096]{1,0:T(8,128)(2,1)} async-done(((bf16[256,256]{1,0:T(8,128)(2,1)}), bf16[256,4096]{1,0:T(8,128)(2,1)}) %all-gather.5.cloned.1.call-update) | async-done | bytes 2097168 | tf_op jit(solution)/shard_map/all_gather | solution.py:39
  125.2 2.5 convolution_convert_fusion
  127.7 59.3 %all-gather.7.cloned.1.call-done = bf16[8192,256]{1,0:T(8,128)(2,1)} async-done(((bf16[256,256]{1,0:T(8,128)(2,1)}), bf16[8192,256]{1,0:T(8,128)(2,1)}) %all-gather.7.cloned.1.call-update) | async-done | bytes 4194320 | tf_op jit(solution)/shard_map/all_gather | solution.py:52
  187.0 6.4 %copy.6 = bf16[8192,256]{0,1:T(8,128)(2,1)} copy(bf16[8192,256]{1,0:T(8,128)(2,1)} %all-gather.7.cloned.1.call-done) | data formatting | bytes 8388608 | tf_op jit(solution)/shard_map/all_gather | solution.py:52
  193.4 15.6 %multiply_reduce_fusion = (f32[4,256]{1,0:T(4,128)S(1)}, f32[4,256,8192]{2,1,0:T(8,128)}) fusion(bf16[256,4,64]{0,2,1:T(8,128)(2,1)S(1)} %bitcast.29, bf16[8192,4,64]{0,2,1:T(8,128)(2,1)} %bitcast.27), kind=kOutput, calls=%fused_computation.1 | convolution fusion | flops 1090518016 | bytes 37883904 | tf_op jit(solution)/shard_map/qhd,khd->hqk/dot_general | solution.py:15
  209.0 44.8 %all-gather.9.cloned.1.call-done = bf16[8192,256]{1,0:T(8,128)(2,1)} async-done(((bf16[256,256]{1,0:T(8,128)(2,1)}), bf16[8192,256]{1,0:T(8,128)(2,1)}) %all-gather.9.cloned.1.call-update) | async-done | bytes 4194320 | tf_op jit(solution)/shard_map/all_gather | solution.py:53
  253.7 6.4 %copy.7 = bf16[8192,256]{0,1:T(8,128)(2,1)} copy(bf16[8192,256]{1,0:T(8,128)(2,1)} %all-gather.9.cloned.1.call-done) | data formatting | bytes 8388608 | tf_op jit(solution)/shard_map/all_gather | solution.py:53
  260.1 14.1 %fusion = f32[4,256]{1,0:T(4,128)S(1)} fusion(f32[4,256,8192]{2,1,0:T(8,128)} %get-tuple-element.6, f32[4,256]{1,0:T(4,128)S(1)} %get-tuple-element.5), kind=kLoop, calls=%fused_computation.2 | loop fusion | flops 25164800 | bytes 33562624 | tf_op jit(solution)/shard_map/reduce_sum | solution.py:21
  274.2 15.5 %fusion.13 = bf16[256,4,64]{0,2,1:T(8,128)(2,1)S(1)} fusion(bf16[8192,4,64]{0,2,1:T(8,128)(2,1)} %bitcast.26, f32[4,256,8192]{2,1,0:T(8,128)} %get-tuple-element.6, f32[4,256]{1,0:T(4,128)S(1)} %get-tuple-element.5, f32[256,4]{0,1:T(4,128)S(1)} %bitcast_add_fusion, f32[256,4]{0,1:T(4,128)S(1)} %multiply_bitcast_fusion), kind=kOutput, calls=%fused_computation.9 | convolution fusion | flops 1099104256 | bytes 37892096 | tf_op jit(solution)/shard_map/hqk,khd->hqd/dot_general | solution.py:22
  289.8 27.8 %all-gather.11.cloned.1.call-done = bf16[4096,256]{1,0:T(8,128)(2,1)} async-done(((bf16[128,256]{1,0:T(8,128)(2,1)}), bf16[4096,256]{1,0:T(8,128)(2,1)}) %all-gather.11.cloned.1.call-update) | async-done | bytes 2097168 | tf_op jit(solution)/shard_map/all_gather | solution.py:57
  317.6 4.3 fusion.17
  321.9 0.0 reduce-scatter.2.cloned.1.call-update
  321.9 239.0 %reduce-scatter.2.cloned.1.call-done = f32[16,4096]{1,0:T(8,128)} async-done(((f32[256,4096]{1,0:T(8,128)}), f32[16,4096]{1,0:T(8,128)}) %reduce-scatter.2.cloned.1.call-update) | async-done | bytes 262160 | tf_op jit(solution)/shard_map/reduce_scatter | solution.py:58
  560.8 1.6 convert_element_type.19
  (4 shorter events, 0.0 us)
Async XLA Ops:
  6.5 118.6 %all-gather.5.cloned.1.call-start = ((), (), s32[]{:S(2)}) async-start(), calls=%async_computation.2 | async-start | bytes 2228224 | tf_op jit(solution)/shard_map/all_gather | solution.py:39
  7.3 179.8 %all-gather.7.cloned.1.call-start = ((), (), s32[]{:S(2)}) async-start(), calls=%async_computation.3 | async-start | bytes 4325376 | tf_op jit(solution)/shard_map/all_gather | solution.py:52
  8.0 245.7 %all-gather.9.cloned.1.call-start = ((), (), s32[]{:S(2)}) async-start(), calls=%async_computation.4 | async-start | bytes 4325376 | tf_op jit(solution)/shard_map/all_gather | solution.py:53
  11.1 114.0 %all-to-all-start = ((bf16[32,128,256]{2,1,0:T(8,128)(2,1)}), bf16[32,128,256]{2,1,0:T(8,128)(2,1)S(1)}, u32[]{:S(2)}, u32[]{:S(2)}) async-start(bf16[32,128,256]{2,1,0:T(8,128)(2,1)} %stack.2), calls=%async_computation | async-start | bytes 4194304 | tf_op jit(solution)/shard_map/all_to_all | solution.py:33
  20.6 296.9 %all-gather.11.cloned.1.call-start = ((), (), s32[]{:S(2)}) async-start(), calls=%async_computation.5 | async-start | bytes 2162688 | tf_op jit(solution)/shard_map/all_gather | solution.py:57
  21.2 539.6 %reduce-scatter.2.cloned.1.call-start = ((), (), s32[]{:S(2)}) async-start(), calls=%async_computation.6 | async-start | bytes 4456448 | tf_op jit(solution)/shard_map/reduce_scatter | solution.py:58
Sparse Core Ops, SparseCore 0:
  10.4 114.6 all-gather.4
  127.3 59.6 all-gather.6
  189.2 64.5 all-gather.8
  255.8 61.7 all-gather.10
  322.0 238.7 reduce-scatter.1
